TPU v7x, 32 devices: a whole 2x2x4 slice. The times are simulated.
32 devices in a mesh: group: 2 (over x), depth: 2 (over core), col: 8 (over z, y).
Axes of the slice: x: 2, y: 2, z: 4, core: 2. Of those that a mesh axis runs over, the one named last changes fastest.
Arguments:
- alignment_activations: bfloat16 [256, 32, 256], P(('group', 'depth'), 'col'), parts along dimension 0, may hold values from -8 to 8
- alignment_mask: int32 [256, 32], P(('group', 'depth'), 'col'), parts along dimension 0, may hold values from 0 to 1, as said below
- pair_activation_input: bfloat16 [64, 32, 128], P(('group', 'col'), 'depth'), parts along dimension 0, may hold values from -6 to 6
- pair_update_mask: int32 [64, 32], P(('group', 'col'), 'depth'), parts along dimension 0, may hold values 0 or 1
- pair_output_gradient: bfloat16 [64, 32, 128], P(('group', 'col'), 'depth'), parts along dimension 0, may hold values from -6 to 6
- layer_scale_factor: float32 [256], replicated, may hold values from 0.25 to 1.75
- first_projector: bfloat16 [256, 32], replicated, may hold values from -0.375 to 0.375
- second_projector: bfloat16 [256, 32], replicated, may hold values from -0.375 to 0.375
- output_weight: bfloat16 [1024, 128], replicated, may hold values from -1.5 to 1.5
- pair_norm_gain: float32 [128], replicated, may hold values from 0.25 to 1.75
- hidden_weight: bfloat16 [128, 512], replicated, may hold values from -0.5 to 0.5
- back_weight: bfloat16 [512, 128], replicated, may hold values from -0.25 to 0.25
Outputs:
- features_derivative: bfloat16 [256, 32, 256], P(('group', 'depth'), 'col'), parts along dimension 0
- couple_features_derivative: bfloat16 [64, 32, 128], P(('group', 'col'), 'depth'), parts along dimension 0
- first_projector_derivative: float32 [512, 32], P('group'), parts along dimension 0
- second_projector_derivative: float32 [512, 32], P('group'), parts along dimension 0
- result_matrix_derivative: float32 [2048, 128], P('group'), parts along dimension 0
- middle_matrix_derivative: float32 [256, 512], P('group'), parts along dimension 0
- final_matrix_derivative: float32 [1024, 128], P('group'), parts along dimension 0
There are 2 independent parts, one for each index of `group`. A program takes and returns all parts, laid end to end along the dimension named above; an argument that names none is the same for every part. Nothing has to cross between parts.
Inputs may be any that keep to these rules, and one draw needn't show every extreme that they name: `alignment_mask`: sequence 0 is present at every residue.
All inputs are finite; a program needn't handle non-finite values. No bound on the sum of `pair_update_mask` on one device may be relied on, other than what follows from the above.
Results may differ from a plain program's by a relative error of at most 0.014.
Values may be sent and summed in bfloat16 or wider, within the bound.
A program may use at most 64 MiB of HBM per device.

v0:
```python
import jax
import jax.numpy as jnp
from jax import lax
from jax.sharding import PartitionSpec as P

epsilon = 1e-05
highest = lax.Precision.HIGHEST


def norm_pieces(entries_drawn):
    center = entries_drawn - jnp.mean(entries_drawn, axis=-1, keepdims=True)
    inv_std = lax.rsqrt(jnp.mean(center * center, axis=-1, keepdims=True) + epsilon)
    return (center * inv_std, inv_std)


def standardize_adjoint(grad_scaled, scaled, inv_std):
    mean_grad = jnp.mean(grad_scaled, axis=-1, keepdims=True)
    mean_cross = jnp.mean(grad_scaled * scaled, axis=-1, keepdims=True)
    return inv_std * (grad_scaled - mean_grad - scaled * mean_cross)


def silu_pieces(pre_act):
    sigma = jax.nn.sigmoid(pre_act)
    return (pre_act * sigma, sigma * (1.0 + pre_act * (1.0 - sigma)))


def on_device(
    alignment_activations,
    alignment_mask,
    pair_activation_input,
    pair_update_mask,
    pair_output_gradient,
    layer_scale_factor,
    first_projector,
    second_projector,
    output_weight,
    pair_norm_gain,
    hidden_weight,
    back_weight,
):
    sequence_row_block, residue_row_block, channel_total = alignment_activations.shape
    proj_width = first_projector.shape[1]
    outer_width = proj_width * proj_width
    depth_count = lax.axis_size("depth")
    residues = residue_row_block * lax.axis_size("col")
    pair_cols = pair_activation_input.shape[1]
    pair_width = pair_activation_input.shape[2]
    col_block = min(64, pair_cols)
    block_count = pair_cols // col_block
    standardized_features, reciprocal_spread = norm_pieces(
        alignment_activations.astype(jnp.float32)
    )
    normalized_rows = (standardized_features * layer_scale_factor).astype(jnp.bfloat16)
    mask_floating = alignment_mask.astype(jnp.float32)
    left_proj = (
        jnp.dot(normalized_rows, first_projector, preferred_element_type=jnp.float32)
        * mask_floating[:, :, None]
    ).astype(jnp.bfloat16)
    right_proj = (
        jnp.dot(normalized_rows, second_projector, preferred_element_type=jnp.float32)
        * mask_floating[:, :, None]
    ).astype(jnp.bfloat16)
    right_flat = right_proj.reshape(sequence_row_block, residue_row_block * proj_width)
    mask_converted = alignment_mask.astype(jnp.bfloat16)
    seq_total = left_proj.shape[0]
    gathered, gathered_mask = (
        lax.all_gather(right_flat, "col", axis=1, tiled=True),
        lax.all_gather(mask_converted, "col", axis=1, tiled=True),
    )
    right_blocks = gathered.reshape(seq_total, depth_count, pair_cols, proj_width)
    mask_blocks = gathered_mask.reshape(seq_total, depth_count, pair_cols)
    block_depth = right_blocks.shape[1]
    out_wide = output_weight.astype(jnp.float32)

    def partial_outer(col_start):
        right_piece = lax.dynamic_slice_in_dim(right_blocks, col_start, col_block, 2)
        outer_part = jnp.einsum(
            "sic,sejd->iejcd", left_proj, right_piece, preferred_element_type=jnp.float32
        )
        return (
            outer_part.reshape(residue_row_block, block_depth, col_block, outer_width),
            right_piece,
        )

    def forward_step(step_index, loop_state):
        projected, pair_count = loop_state
        col_start = step_index * col_block
        outer_part, right_piece = partial_outer(col_start)
        mask_piece = lax.dynamic_slice_in_dim(mask_blocks, col_start, col_block, 2).astype(
            jnp.float32
        )
        count_part = jnp.einsum("si,sej->iej", mask_floating, mask_piece, precision=highest)
        outer_mine, count_mine = (
            lax.psum_scatter(
                outer_part.astype(jnp.bfloat16), "depth", scatter_dimension=1, tiled=True
            ).astype(jnp.float32),
            lax.psum_scatter(
                count_part.astype(jnp.bfloat16), "depth", scatter_dimension=1, tiled=True
            ).astype(jnp.float32),
        )
        proj_mine = jnp.dot(
            outer_mine.reshape(residue_row_block * col_block, outer_width),
            out_wide,
            precision=highest,
        )
        proj_mine = proj_mine.reshape(residue_row_block, col_block, pair_width)
        count_mine = count_mine.reshape(residue_row_block, col_block)
        projected = lax.dynamic_update_slice_in_dim(projected, proj_mine, col_start, 1)
        pair_count = lax.dynamic_update_slice_in_dim(pair_count, count_mine, col_start, 1)
        return (projected, pair_count)

    projected, pair_count = lax.fori_loop(
        0,
        block_count,
        forward_step,
        (
            jnp.zeros((residue_row_block, pair_cols, pair_width), jnp.float32),
            jnp.zeros((residue_row_block, pair_cols), jnp.float32),
        ),
    )
    count_column = pair_count.reshape(residue_row_block * pair_cols, 1)
    mid_act = (
        pair_activation_input.reshape(residue_row_block * pair_cols, pair_width).astype(jnp.float32)
        + projected.reshape(residue_row_block * pair_cols, pair_width) / count_column
    )
    pair_scaled, pair_inv = norm_pieces(mid_act)
    pair_normed = (pair_scaled * pair_norm_gain).astype(jnp.bfloat16)
    pre_act = jnp.dot(pair_normed, hidden_weight, preferred_element_type=jnp.float32)
    act_value, act_slope = silu_pieces(pre_act)
    hidden = act_value.astype(jnp.bfloat16)
    masked_grad = (
        pair_output_gradient * pair_update_mask.astype(jnp.bfloat16)[:, :, None]
    ).reshape(residue_row_block * pair_cols, pair_width)
    final_matrix_derivative = jnp.dot(hidden.T, masked_grad, preferred_element_type=jnp.float32)
    back_prod = jnp.dot(masked_grad, back_weight.T, preferred_element_type=jnp.float32)
    grad_hidden = (back_prod * act_slope).astype(jnp.bfloat16)
    middle_matrix_derivative = jnp.dot(
        pair_normed.T, grad_hidden, preferred_element_type=jnp.float32
    )
    grad_scaled = (
        jnp.dot(grad_hidden, hidden_weight.T, preferred_element_type=jnp.float32) * pair_norm_gain
    )
    grad_mid = pair_output_gradient.reshape(residue_row_block * pair_cols, pair_width).astype(
        jnp.float32
    ) + standardize_adjoint(grad_scaled, pair_scaled, pair_inv)
    couple_features_derivative = grad_mid.astype(jnp.bfloat16).reshape(
        residue_row_block, pair_cols, pair_width
    )
    grad_opm = (
        (grad_mid / count_column)
        .astype(jnp.bfloat16)
        .reshape(residue_row_block, pair_cols, pair_width)
    )
    full_opm = lax.all_gather(grad_opm, "depth", axis=1, tiled=True).reshape(
        residue_row_block, depth_count, pair_cols, pair_width
    )

    def backward_step(step_index, loop_state):
        grad_left_acc, grad_out, right_term = loop_state
        col_start = step_index * col_block
        outer_part, right_piece = partial_outer(col_start)
        opm_piece = lax.dynamic_slice_in_dim(full_opm, col_start, col_block, 2).reshape(
            residue_row_block * block_depth * col_block, pair_width
        )
        grad_out = grad_out + jnp.dot(
            outer_part.reshape(residue_row_block * block_depth * col_block, outer_width).T,
            opm_piece.astype(jnp.float32),
            precision=highest,
        )
        grad_outer = jnp.dot(opm_piece, output_weight.T, preferred_element_type=jnp.float32).astype(
            jnp.bfloat16
        )
        grad_outer = grad_outer.reshape(
            residue_row_block, block_depth, col_block, proj_width, proj_width
        )
        grad_left_acc = grad_left_acc + jnp.einsum(
            "iejcd,sejd->sic", grad_outer, right_piece, preferred_element_type=jnp.float32
        )
        piece_term = jnp.einsum(
            "iejcd,sic->ejsd", grad_outer, left_proj, preferred_element_type=jnp.float32
        )
        piece_term = piece_term.reshape(block_depth, col_block, seq_total * proj_width)
        right_term = lax.dynamic_update_slice_in_dim(right_term, piece_term, col_start, 1)
        return (grad_left_acc, grad_out, right_term)

    grad_left_acc, result_matrix_derivative, right_term = lax.fori_loop(
        0,
        block_count,
        backward_step,
        (
            jnp.zeros((seq_total, residue_row_block, proj_width), jnp.float32),
            jnp.zeros((outer_width, pair_width), jnp.float32),
            jnp.zeros((block_depth, pair_cols, seq_total * proj_width), jnp.float32),
        ),
    )
    grad_right_sum = lax.psum_scatter(
        right_term.reshape(residues, seq_total * proj_width), "col", scatter_dimension=0, tiled=True
    )
    grad_right_acc = jnp.transpose(
        grad_right_sum.reshape(residue_row_block, seq_total, proj_width), (1, 0, 2)
    )
    grad_left = (grad_left_acc * mask_floating[:, :, None]).astype(jnp.bfloat16)
    grad_right = (grad_right_acc * mask_floating[:, :, None]).astype(jnp.bfloat16)
    normed_rows = normalized_rows.reshape(sequence_row_block * residue_row_block, channel_total)
    first_projector_derivative = jnp.dot(
        normed_rows.T,
        grad_left.reshape(sequence_row_block * residue_row_block, proj_width),
        preferred_element_type=jnp.float32,
    )
    second_projector_derivative = jnp.dot(
        normed_rows.T,
        grad_right.reshape(sequence_row_block * residue_row_block, proj_width),
        preferred_element_type=jnp.float32,
    )
    standardized_derivative = jnp.dot(
        grad_left, first_projector.T, preferred_element_type=jnp.float32
    ) + jnp.dot(grad_right, second_projector.T, preferred_element_type=jnp.float32)
    features_derivative = standardize_adjoint(
        standardized_derivative * layer_scale_factor, standardized_features, reciprocal_spread
    ).astype(jnp.bfloat16)
    weight_sums = lax.psum(
        (
            first_projector_derivative,
            second_projector_derivative,
            result_matrix_derivative,
            middle_matrix_derivative,
            final_matrix_derivative,
        ),
        ("depth", "col"),
    )
    return (
        features_derivative,
        couple_features_derivative,
        weight_sums[0],
        weight_sums[1],
        weight_sums[2],
        weight_sums[3],
        weight_sums[4],
    )


def solution(mesh):
    in_specs = (
        P(("group", "depth"), "col", None),
        P(("group", "depth"), "col"),
        P(("group", "col"), "depth", None),
        P(("group", "col"), "depth"),
        P(("group", "col"), "depth", None),
        P(),
        P(),
        P(),
        P(),
        P(),
        P(),
        P(),
    )
    out_specs = (
        P(("group", "depth"), "col", None),
        P(("group", "col"), "depth", None),
        P("group", None),
        P("group", None),
        P("group", None),
        P("group", None),
        P("group", None),
    )
    return jax.shard_map(
        on_device, mesh=mesh, in_specs=in_specs, out_specs=out_specs, check_vma=False
    )
```

profile of v0, /device:TPU:0, one launch (start us, length us, event | category | flops | bytes accessed | tf_op | source)
XLA Modules:
  0.0 362.0 jit_solution(7298277247969911914)
XLA Ops:
  7.2 0.0 all-reduce.10.cloned.1.call-start
  7.2 1.0 convert_reduce_fusion
  8.3 1.1 fusion.16
  9.4 0.8 convert_bitcast_fusion
  10.2 1.2 fusion.4
  11.3 32.6 %all_gather.9 = bf16[64,1024]{0,1:T(8,128)(2,1)S(1)} all-gather(bf16[64,128]{0,1:T(8,128)(2,1)S(1)} %bitcast.138), channel_id=1, replica_groups=mesh['group'=2,'depth'=2,'col'=8] {'col'}, dimensions={1}, use_global_device_ids=true | all-gather | bytes 147456 | tf_op jit(solution)/shard_map/all_gather | solution.py:67
  43.9 1.2 fusion.5
  45.1 1.8 fusion.45
  46.9 0.6 copy.30
  47.5 1.9 convert_element_type.96
  49.4 0.0 all-reduce.10.cloned.1.call-update
  49.4 0.0 all-reduce.12.cloned.1.call-start
  49.5 20.6 %all-gather = bf16[8,4,64]{2,1,0:T(4,128)(2,1)S(1)} all-gather(bf16[1,4,64]{2,1,0:T(4,128)(2,1)S(1)} %get-tuple-element.95), channel_id=1, replica_groups=mesh['group'=2,'depth'=2,'col'=8] {'col'}, dimensions={0}, use_global_device_ids=true | all-gather | bytes 4608 | tf_op jit(solution)/shard_map/all_gather | solution.py:68
  70.0 0.1 convolution_convert_fusion.1
  70.2 2.5 all-reduce.1
  72.7 0.6 dynamic-slice
  73.3 0.7 dynamic-slice_convert_fusion
  73.9 0.1 div.60
  74.0 0.6 dynamic-slice.4
  74.6 1.9 copy.35
  76.6 1.0 reshape.170
  78.2 0.1 broadcast_multiply_fusion
  78.3 1.6 constant_dynamic-slice_fusion.1
  79.9 0.2 fusion.46
  80.1 0.2 fusion.33
  80.3 0.1 div.63
  80.3 0.2 multiply_reduce_fusion.1
  80.5 0.1 rsqrt.21
  80.6 0.1 fusion.23
  80.7 0.1 fusion.32
  80.9 0.2 fusion.1
  81.1 0.3 fusion.43
  81.3 0.9 fusion.31
  82.3 0.9 fusion.17
  83.2 0.7 fusion.44
  83.9 0.1 divide_convert_fusion
  84.0 1.8 all_gather.11
  85.8 0.2 convolution_convert_fusion
  86.1 0.8 reshape.166
  86.9 0.4 convolution_bitcast_fusion.1
  87.3 0.4 fusion.3
  87.7 0.4 copy.33
  88.1 1.2 reshape.167
  89.3 0.0 all-reduce.14.cloned.1.call-start
  89.4 0.9 convolution_bitcast_fusion.4
  90.3 1.4 fusion.47
  91.7 66.1 %all-reduce.12.cloned.1.call-done = f32[32,2048]{1,0:T(8,128)} async-done(((f32[32,2048]{1,0:T(8,128)}), f32[32,2048]{1,0:T(8,128)}) %all-reduce.12.cloned.1.call-update) | async-done | bytes 262160
  157.8 0.8 constant_dynamic-slice_fusion
  158.6 0.1 reshape.168
  158.7 0.1 copy.34
  158.8 0.9 convolution_bitcast_fusion.3
  159.7 0.0 all-reduce.16.cloned.1.call-start
  159.8 0.2 fusion.24
  160.0 0.3 all-reduce.16.cloned.1.call-update
  160.3 0.3 fusion.42
  160.7 0.2 fusion.15
  160.9 0.8 copy.36
  161.7 85.9 %all-reduce.14.cloned.1.call-done = (f32[256,32]{0,1:T(8,128)}, f32[256,32]{0,1:T(8,128)}) async-done(((f32[256,32]{0,1:T(8,128)}, f32[256,32]{0,1:T(8,128)}), (f32[256,32]{0,1:T(8,128)}, f32[256,32]{0,1:T(8,128)})) %all-reduce.14.cloned.1.call-update) | async-done | bytes 65552 | tf_op jit(solution)/shard_map/psum | solution.py:221
  247.6 99.9 %all-reduce.16.cloned.1.call-done = (f32[1024,128]{1,0:T(8,128)}, f32[128,512]{1,0:T(8,128)}, f32[512,128]{1,0:T(8,128)}) async-done(((f32[1024,128]{1,0:T(8,128)}, f32[128,512]{1,0:T(8,128)}, f32[512,128]{1,0:T(8,128)}), (f32[1024,128]{1,0:T(8,128)}, f32[128,512]{1,0:T(8,128)}, f32[512,128]{1,0:T(8,128)})) %all-reduce.16.cloned.1.call-update) | async-done | bytes 1048592 | tf_op jit(solution)/shard_map/psum | solution.py:221
  347.5 1.4 copy.62
  348.9 1.4 copy.63
  350.3 1.9 copy.64
  352.1 1.7 copy.65
  353.8 1.7 copy.66
  (39 shorter events, 0.2 us)
Async XLA Ops:
  7.2 72.7 %copy-start = (bf16[1024,128]{1,0:T(8,128)(2,1)S(1)}, bf16[1024,128]{1,0:T(8,128)(2,1)}, u32[]{:S(2)}) copy-start(bf16[1024,128]{1,0:T(8,128)(2,1)} %param.20) | copy-start | bytes 786436
  7.2 71.1 %all-reduce.10.cloned.1.call-start = ((), (), s32[]{:S(2)}) async-start(), calls=%async_computation | async-start | bytes 524288
  46.9 23.2 %copy-start.7 = (s32[64,4]{0,1:T(4,128)S(1)}, s32[64,4]{0,1:T(4,128)}, u32[]{:S(2)}) copy-start(s32[64,4]{0,1:T(4,128)} %param.13) | copy-start | bytes 3076
  46.9 25.8 %copy-start.13 = (u32[32]{0:T(128)S(1)}, u32[32]{0:T(128)}, u32[]{:S(2)}) copy-start(u32[32]{0:T(128)} %constant.47) | copy-start | bytes 388
  46.9 27.2 %copy-start.9 = (s32[4,16]{1,0:T(4,128)S(1)}, s32[4,16]{1,0:T(4,128)}, u32[]{:S(2)}) copy-start(s32[4,16]{1,0:T(4,128)} %param.15) | copy-start | bytes 772
  46.9 27.2 %copy-start.12 = (u32[32]{0:T(128)S(1)}, u32[32]{0:T(128)}, u32[]{:S(2)}) copy-start(u32[32]{0:T(128)} %constant.55) | copy-start | bytes 388
  49.4 108.4 %all-reduce.12.cloned.1.call-start = ((), (), s32[]{:S(2)}) async-start(), calls=%async_computation.1 | async-start | bytes 524288
  76.6 1.7 copy-start.4
  76.6 3.5 copy-start.3
  76.6 4.2 %copy-start.2 = (bf16[128,512]{1,0:T(8,128)(2,1)S(1)}, bf16[128,512]{1,0:T(8,128)(2,1)}, u32[]{:S(2)}) copy-start(bf16[128,512]{1,0:T(8,128)(2,1)} %param.22) | copy-start | bytes 393220
  76.6 4.1 %copy-start.8 = (f32[128]{0:T(128)S(1)}, f32[128]{0:T(128)}, u32[]{:S(2)}) copy-start(f32[128]{0:T(128)} %param.21) | copy-start | bytes 1540
  76.6 4.3 %copy-start.11 = (bf16[512,128]{1,0:T(8,128)(2,1)S(1)}, bf16[512,128]{1,0:T(8,128)(2,1)}, u32[]{:S(2)}) copy-start(bf16[512,128]{1,0:T(8,128)(2,1)} %param.23) | copy-start | bytes 393220
  87.3 2.1 copy-start.1
  87.3 2.1 copy-start.10
  88.1 71.7 %copy-start.5 = (bf16[256,32]{0,1:T(8,128)(2,1)S(1)}, bf16[256,32]{0,1:T(8,128)(2,1)}, u32[]{:S(2)}) copy-start(bf16[256,32]{0,1:T(8,128)(2,1)} %param.18) | copy-start | bytes 49156
  89.3 71.0 %copy-start.6 = (bf16[256,32]{0,1:T(8,128)(2,1)S(1)}, bf16[256,32]{0,1:T(8,128)(2,1)}, u32[]{:S(2)}) copy-start(bf16[256,32]{0,1:T(8,128)(2,1)} %param.19) | copy-start | bytes 49156
  89.3 158.3 %all-reduce.14.cloned.1.call-start = ((), (), s32[]{:S(2)}) async-start(), calls=%async_computation.2 | async-start | bytes 131072 | tf_op jit(solution)/shard_map/psum | solution.py:221
  159.7 187.8 %all-reduce.16.cloned.1.call-start = ((), (), s32[]{:S(2)}) async-start(), calls=%async_computation.3 | async-start | bytes 2097152 | tf_op jit(solution)/shard_map/psum | solution.py:221
Sparse Core Ops, SparseCore 0:
  49.5 19.2 all-reduce.9
  89.5 68.2 all-reduce.11
  161.9 85.6 all-reduce.13
  251.8 95.6 all-reduce.15
where the time goes:
time: 363 us; the launch traced here: 362 us
  waiting for transfers between devices  252 us (69%)
  blocking collectives  57.5 us (16%)
  local copies, waits for them, and re-layouts  20.5 us (6%)
  between operations  14.8 us (4%)
  matrix products  11.6 us (3%)
  other arithmetic  5.09 us (1%)
    psum x2, waiting for transfers between devices, on_device(): lax.psum((first_projector_derivative, second_projector_derivative, result...  186 us
    unnamed x6, waiting for transfers between devices  66.5 us
    all_gather x1, blocking collectives, on_device(): lax.all_gather(right_flat, 'col', axis=1, tiled=True)  32.6 us
    all_gather x1, blocking collectives, on_device(): lax.all_gather(mask_converted, 'col', axis=1, tiled=True)  20.6 us
    unnamed x38, local copies, waits for them, and re-layouts  12.4 us
  transfers between devices with their start and end apart: 4, of which 3 were waited for; matrix products, arithmetic and copies ran while one was open for 2% of the time, Pallas kernels for 0%

commit v1 on v0

v1 whole, which is shorter than its diff:
```python
import functools

import jax
import jax.numpy as jnp
from jax import lax
from jax.experimental import pallas as pl
from jax.experimental.pallas import tpu as pltpu
from jax.sharding import PartitionSpec as P

EPS = 1e-05
F32 = jnp.float32
BF16 = jnp.bfloat16
MESH = pl.DeviceIdType.MESH


def mm(a, b, ca=1, cb=0):
    return lax.dot_general(a, b, (((ca,), (cb,)), ((), ())), preferred_element_type=F32)


def norm_pieces(v):
    center = v - jnp.mean(v, axis=-1, keepdims=True)
    inv = lax.rsqrt(jnp.mean(center * center, axis=-1, keepdims=True) + EPS)
    return center * inv, inv


def standardize_adjoint(g, scaled, inv):
    mean_g = jnp.mean(g, axis=-1, keepdims=True)
    mean_c = jnp.mean(g * scaled, axis=-1, keepdims=True)
    return inv * (g - mean_g - scaled * mean_c)


def iota(shape, axis):
    return lax.broadcasted_iota(jnp.int32, shape, axis)


def kernel(
    ncol, seqs, res, cols, cw,
    x_ref, am_ref, pin_ref, pm_ref, pg_ref, ls_ref, fp_ref, sp_ref, ow_ref, png_ref, hw_ref, bw_ref,
    feat_ref, couple_ref, wsum_ref, small_ref,
    lbuf, rbuf, mloc, mrow, mcol, lsend, rsend,
    outer, gbuf, scaled_sc, normed_sc,
    grsend, grrecv, glsend, glrecv,
    wb, w1recv, w1s, w2recv, w3, wout,
    sm, srecv, smine, sout,
    sem_l, sem_r, sem_ml, sem_mr, sem_gr, sem_gl, sem_w1, sem_w2, sem_w3, sem_w4, sem_s1, sem_s2,
    snd_l, snd_r, snd_ml, snd_mr, snd_gr, snd_gl, snd_w1, snd_w2, snd_w3, snd_w4, snd_s1, snd_s2,
):
    g = lax.axis_index("group")
    e = lax.axis_index("depth")
    k = lax.axis_index("col")
    f = 1 - e
    n = 2 * ncol
    me = e * ncol + k
    lanes = res * cw
    jts = cols // res
    grp = lanes // cw
    cts = cw // grp
    pairs = res * cols
    z = pin_ref.shape[1]

    barrier = pltpu.get_barrier_semaphore()
    for t in range(1, n):
        peer = lax.rem(me + t, n)
        pl.semaphore_signal(
            barrier, inc=1, device_id=(g, lax.div(peer, ncol), lax.rem(peer, ncol)),
            device_id_type=MESH,
        )

    def rcopy(src, dst, ssem, rsem, d, c):
        return pltpu.make_async_remote_copy(
            src_ref=src, dst_ref=dst, send_sem=ssem, recv_sem=rsem,
            device_id=(g, d, c), device_id_type=MESH,
        )

    scaled, inv = norm_pieces(x_ref[...].astype(F32))
    normed = (scaled * ls_ref[...]).astype(BF16)
    scaled_sc[...] = scaled
    normed_sc[...] = normed
    el_c = iota((cw, lanes), 0)
    el_l = iota((cw, lanes), 1)
    expand_l = (grp * lax.div(lax.rem(el_l, cw), res) + lax.div(el_l, cw) == el_c).astype(F32).astype(BF16)
    expand_r = (lax.rem(el_l, cw) == el_c).astype(F32).astype(BF16)
    wl = mm(fp_ref[...], expand_l).astype(BF16)
    wr = mm(sp_ref[...], expand_r).astype(BF16)
    pl_full = mm(normed, wl)
    pr_full = mm(normed, wr)
    ln = iota((seqs, lanes), 1)
    res_l = lax.rem(ln, res)
    res_r = lax.div(ln, cw)
    mask = am_ref[...].astype(F32)
    zero = jnp.zeros((seqs, lanes), F32)
    left, right, ml, mr, mpad = zero, zero, zero, zero, zero
    for r in range(res):
        col = jnp.broadcast_to(mask[:, r : r + 1], (seqs, lanes))
        left = jnp.where(res_l == r, pl_full[r * seqs : (r + 1) * seqs], left)
        right = jnp.where(res_r == r, pr_full[r * seqs : (r + 1) * seqs], right)
        ml = jnp.where(res_l == r, col, ml)
        mr = jnp.where(res_r == r, col, mr)
        mpad = jnp.where(ln == r, col, mpad)
    left = (left * ml).astype(BF16)
    right = (right * mr).astype(BF16)
    lsend[...] = left
    rsend[...] = right
    lbuf[e] = left
    eye = (iota((seqs, lanes), 0) == ln).astype(F32).astype(BF16)
    mt = mm(mpad.astype(BF16), eye, 0, 0)[0:8]
    mloc[...] = mt
    mrow[e] = mt
    own_e = lax.div(k, jts)
    own_jt = lax.rem(k, jts)

    pl.semaphore_wait(barrier, n - 1)

    c_left = rcopy(lsend, lbuf.at[e], snd_l, sem_l, f, k)
    c_ml = rcopy(mloc, mrow.at[e], snd_ml, sem_ml, f, k)

    def r_copies(t):
        kk = lax.rem(k + t, ncol)
        return (
            rcopy(rsend, rbuf.at[own_jt, e], snd_r.at[t], sem_r.at[own_jt, e], own_e, kk),
            rcopy(mloc, mcol.at[e, own_jt], snd_mr.at[t], sem_mr.at[own_jt, e], own_e, kk),
        )

    for t in range(1, ncol):
        for c in r_copies(t):
            c.start()

    @pl.when(own_e == e)
    def _():
        rbuf[own_jt, e] = right
        mcol[e, own_jt] = mt

    @pl.when(own_e != e)
    def _():
        for c in r_copies(0):
            c.start()

    c_left.start()
    c_ml.start()

    pgrad = pg_ref[...]
    sw_r = iota((pairs, pairs), 0)
    sw_c = iota((pairs, pairs), 1)
    swap = (lax.rem(sw_r, res) * cols + lax.div(sw_r, res) == sw_c).astype(F32).astype(BF16)
    pact = mm(swap, pin_ref[...])
    pgrad = mm(swap, pgrad)
    pick = (lax.rem(iota((pairs, res), 0), res) == iota((pairs, res), 1)).astype(F32).astype(BF16)
    prow = mm(pick, pm_ref[...].astype(F32).astype(BF16))
    pj_at = lax.div(iota((pairs, cols), 0), res) == iota((pairs, cols), 1)
    pcol = jnp.sum(jnp.where(pj_at, prow, 0.0), axis=1, keepdims=True)
    masked_grad = (pgrad * pcol).astype(BF16)
    back_prod = mm(masked_grad, bw_ref[...], 1, 1)

    c_left.wait()
    c_ml.wait()
    for jt in range(jts):
        for h in range(2):

            @pl.when(jnp.logical_or(own_e != e, jnp.logical_or(own_jt != jt, e != h)))
            def _():
                rcopy(rsend, rbuf.at[jt, h], snd_r.at[0], sem_r.at[jt, h], e, k).wait_recv()
                rcopy(mloc, mcol.at[h, jt], snd_mr.at[0], sem_mr.at[jt, h], e, k).wait_recv()

    pi = (lax.rem(iota((pairs, 8), 0), res) == iota((pairs, 8), 1)).astype(F32).astype(BF16)
    pj_r = lax.div(iota((pairs, jts * 8), 0), res)
    pj_l = iota((pairs, jts * 8), 1)
    pj = jnp.logical_and(
        lax.div(pj_r, res) == lax.div(pj_l, 8), lax.rem(pj_r, res) == lax.rem(pj_l, 8)
    ).astype(F32).astype(BF16)
    prod = jnp.zeros((pairs, lanes), F32)
    for h in range(2):
        mi = mm(pi, mrow[h].astype(BF16))
        mj = mm(pj, mcol[h].reshape(jts * 8, lanes).astype(BF16))
        prod = prod + mi * mj
    count = jnp.sum(prod, axis=1, keepdims=True)

    lall = lbuf[...].reshape(2 * seqs, lanes)
    atom = lax.div(iota((cw, lanes), 1), cw)
    top = lax.rem(iota((cw, lanes), 0), 2 * res) < res
    for jt in range(jts):
        o = mm(lall, rbuf[jt].reshape(2 * seqs, lanes), 0, 0)
        ts = []
        for q in range(grp):
            t_q = o[0:cw]
            if q:
                t_q = pltpu.roll(t_q, (cw * (0 - q)) % lanes, 1)
            for p in range(1, grp):
                v = o[p * cw : (p + 1) * cw]
                if p != q:
                    v = pltpu.roll(v, (cw * (p - q)) % lanes, 1)
                t_q = jnp.where(atom == p, v, t_q)
            ts.append(t_q)
        for q in range(0, grp, 2):
            even = jnp.where(top, ts[q], pltpu.roll(ts[q + 1], res, 0))
            odd = jnp.where(top, pltpu.roll(ts[q], cw - res, 0), ts[q + 1])
            at = (jt * res + q) * res
            for m in range(cts // 2):
                outer[2 * m, at : at + 2 * res, :] = even[m * 2 * res : (m + 1) * 2 * res]
                outer[2 * m + 1, at : at + 2 * res, :] = odd[m * 2 * res : (m + 1) * 2 * res]
    outer_b = jnp.concatenate([outer[ct].astype(BF16) for ct in range(cts)], axis=1)
    projected = mm(outer_b, ow_ref[...])

    mid_act = pact + projected / count
    pscaled, pinv = norm_pieces(mid_act)
    pnormed = (pscaled * png_ref[...]).astype(BF16)
    pre = mm(pnormed, hw_ref[...])
    sig = jax.nn.sigmoid(pre)
    hidden = (pre * sig).astype(BF16)
    grad_hidden = (back_prod * (sig * (1.0 + pre * (1.0 - sig)))).astype(BF16)
    gs = mm(grad_hidden, hw_ref[...], 1, 1) * png_ref[...]
    grad_mid = pgrad + standardize_adjoint(gs, pscaled, pinv)
    couple_ref[...] = mm(swap, grad_mid.astype(BF16), 0, 0).astype(BF16)
    opm = (grad_mid / count).astype(BF16)

    rows = wb.shape[2]
    g_out = mm(opm, ow_ref[...], 1, 1)
    tall = 2 * res
    perm_r = iota((cts * tall, cts * tall), 0)
    perm_c = iota((cts * tall, cts * tall), 1)
    perm_q = lax.div(perm_r, cw)
    perm_t = lax.div(lax.rem(perm_r, cw), res)
    perm = (perm_t * tall + perm_q * res + lax.rem(perm_r, res) == perm_c).astype(F32).astype(BF16)
    stack = jnp.concatenate(
        [
            jnp.concatenate(
                [
                    g_out[b * tall : (b + 1) * tall, ct * lanes : (ct + 1) * lanes]
                    for b in range(pairs // tall)
                ],
                axis=1,
            )
            for ct in range(cts)
        ],
        axis=0,
    )
    moved = mm(perm, stack.astype(BF16))
    gl = jnp.zeros((2 * seqs, lanes), F32)
    for jt in range(jts):
        us = []
        gps = []
        for q in range(grp):
            b = jt * (grp // 2) + q // 2
            us.append(moved[(q % 2) * cw : (q % 2 + 1) * cw, b * lanes : (b + 1) * lanes])
        for p in range(grp):
            g_p = us[0]
            if p:
                g_p = pltpu.roll(g_p, (cw * (0 - p)) % lanes, 1)
            for q in range(1, grp):
                v = us[q]
                if p != q:
                    v = pltpu.roll(v, (cw * (q - p)) % lanes, 1)
                g_p = jnp.where(atom == q, v, g_p)
            gps.append(g_p)
        gj = jnp.concatenate(gps, axis=0).astype(BF16)
        gl = gl + mm(rbuf[jt].reshape(2 * seqs, lanes), gj, 1, 1)
        gr = mm(lall, gj).astype(BF16)
        for h in range(2):
            grsend[h, jt] = gr[h * seqs : (h + 1) * seqs]

    for jt in range(jts):
        for h in range(2):
            owner = e * jts + jt
            here = jnp.logical_and(e == h, owner == k)

            @pl.when(here)
            def _():
                pltpu.make_async_copy(grsend.at[h, jt], grrecv.at[k], sem_gr.at[k]).start()

            @pl.when(jnp.logical_not(here))
            def _():
                rcopy(grsend.at[h, jt], grrecv.at[k], snd_gr.at[h, jt], sem_gr.at[k], h, owner).start()

    gbuf_l = jnp.where(e == 0, gl[seqs:], gl[:seqs])
    gl_own = jnp.where(e == 0, gl[:seqs], gl[seqs:])
    glsend[...] = gbuf_l
    c_gl = rcopy(glsend, glrecv, snd_gl, sem_gl, f, k)
    c_gl.start()

    d_out = mm(outer_b, opm, 0, 0).astype(BF16)
    d_mid = mm(pnormed, grad_hidden, 0, 0).astype(BF16)
    d_fin = mm(hidden, masked_grad, 0, 0).astype(BF16)
    wb[0] = d_out.reshape(ncol, rows, z)
    per = z // rows
    for b in range(d_mid.shape[1] // z):
        wb[1, b * per : (b + 1) * per] = d_mid[:, b * z : (b + 1) * z].reshape(per, rows, z)
    half = (d_mid.shape[1] // z) * per
    wb[1, half:] = d_fin.reshape(ncol - half, rows, z)
    c_w1 = rcopy(wb.at[f], w1recv, snd_w1, sem_w1, f, k)
    c_w1.start()
    c_w1.wait()
    w1s[...] = (wb[e].astype(F32) + w1recv[...].astype(F32)).astype(BF16)

    def w2_copy(t):
        kk = lax.rem(k + t, ncol)
        return rcopy(w1s.at[kk], w2recv.at[k], snd_w2.at[t], sem_w2.at[k], e, kk)

    for t in range(1, ncol):
        w2_copy(t).start()
    w2recv[k] = w1s[k]

    c_gl.wait()
    grad_l = ((gl_own + glrecv[...]) * ml).astype(BF16).astype(F32)
    for kk in range(ncol):
        rcopy(grsend.at[0, 0], grrecv.at[kk], snd_gr.at[0, 0], sem_gr.at[kk], e, k).wait_recv()

    gr_sum = grrecv[0].astype(F32)
    for kk in range(1, ncol):
        gr_sum = gr_sum + grrecv[kk].astype(F32)
    grad_r = (gr_sum * mr).astype(BF16).astype(F32)
    tw = 2 * cw
    fold_l = iota((lanes, 2 * tw), 0)
    fold_c = iota((lanes, 2 * tw), 1)
    c_of = grp * lax.div(lax.rem(fold_l, cw), res) + lax.div(fold_l, cw)
    sel_l = (c_of == lax.rem(fold_c, tw)).astype(F32).astype(BF16)
    sel_r = (lax.rem(fold_l, cw) + cw == lax.rem(fold_c, tw)).astype(F32).astype(BF16)
    gf = []
    for r in range(res):
        a = jnp.where(res_l == r, grad_l, 0.0).astype(BF16)
        b = jnp.where(res_r == r, grad_r, 0.0).astype(BF16)
        gf.append(mm(a, sel_l) + mm(b, sel_r))
    gfold = jnp.concatenate(gf, axis=0)
    low = iota(gfold.shape, 1) < tw
    ga = jnp.where(low, gfold, 0.0).astype(BF16)
    gb = jnp.where(low, 0.0, gfold).astype(BF16)
    nrm = normed_sc[...]
    ch = nrm.shape[1] // 2
    d12 = mm(nrm[:, :ch], ga, 0, 0) + mm(nrm[:, ch:], gb, 0, 0)
    sm[...] = d12.reshape(sm.shape)

    def s1_copy(t):
        peer = lax.rem(me + t, n)
        return rcopy(
            sm.at[peer], srecv.at[me], snd_s1.at[t], sem_s1.at[me],
            lax.div(peer, ncol), lax.rem(peer, ncol),
        )

    for t in range(1, n):
        s1_copy(t).start()
    srecv[me] = sm[me]

    for kk in range(ncol):

        @pl.when(k != kk)
        def _():
            rcopy(w1s.at[0], w2recv.at[kk], snd_w2.at[0], sem_w2.at[kk], e, k).wait_recv()

    acc = w2recv[0].astype(F32)
    for kk in range(1, ncol):
        acc = acc + w2recv[kk].astype(F32)
    w3[...] = acc.astype(BF16)
    wout[e, k] = acc.astype(BF16)

    def w3_copy(t):
        kk = lax.rem(k + t, ncol)
        return rcopy(w3, wout.at[e, k], snd_w3.at[t], sem_w3.at[k], e, kk)

    for t in range(1, ncol):
        w3_copy(t).start()

    def w4_copy(kk):
        return rcopy(wout.at[e, kk], wout.at[e, kk], snd_w4.at[kk], sem_w4.at[kk], f, k)

    w4_own = rcopy(w3, wout.at[e, k], snd_w4.at[k], sem_w4.at[k], f, k)
    w4_own.start()

    nn = mm(ga[:, :cw], fp_ref[...], 1, 1) + mm(ga[:, cw:tw], sp_ref[...], 1, 1)
    feat_ref[...] = standardize_adjoint(nn * ls_ref[...], scaled_sc[...], inv).astype(BF16)

    for p in range(n):

        @pl.when(me != p)
        def _():
            rcopy(sm.at[0], srecv.at[p], snd_s1.at[0], sem_s1.at[p], e, k).wait_recv()

    tot = srecv[0]
    for p in range(1, n):
        tot = tot + srecv[p]
    smine[...] = tot
    sout[me] = tot

    def s2_copy(t):
        peer = lax.rem(me + t, n)
        return rcopy(
            smine, sout.at[me], snd_s2.at[t], sem_s2.at[me],
            lax.div(peer, ncol), lax.rem(peer, ncol),
        )

    for t in range(1, n):
        s2_copy(t).start()

    for t in range(1, ncol):
        kk = lax.rem(k + t, ncol)
        rcopy(w3, wout.at[e, kk], snd_w3.at[0], sem_w3.at[kk], e, k).wait_recv()
        w4_copy(kk).start()

    for p in range(n):

        @pl.when(me != p)
        def _():
            rcopy(smine, sout.at[p], snd_s2.at[0], sem_s2.at[p], e, k).wait_recv()

    small_ref[...] = sout[...].reshape(small_ref.shape)
    for kk in range(ncol):
        rcopy(wout.at[f, kk], wout.at[f, kk], snd_w4.at[kk], sem_w4.at[kk], f, k).wait_recv()
    wsum_ref[...] = wout[...].reshape(wsum_ref.shape)

    for t in range(1, ncol):
        for c in r_copies(t):
            c.wait_send()
        w2_copy(t).wait_send()
        w3_copy(t).wait_send()

    @pl.when(own_e != e)
    def _():
        for c in r_copies(0):
            c.wait_send()

    for jt in range(jts):
        for h in range(2):

            @pl.when(jnp.logical_or(e != h, e * jts + jt != k))
            def _():
                rcopy(grsend.at[h, jt], grrecv.at[k], snd_gr.at[h, jt], sem_gr.at[k], f, k).wait_send()

    for t in range(1, n):
        s1_copy(t).wait_send()
        s2_copy(t).wait_send()
    for kk in range(ncol):
        w4_copy(kk).wait_send()


def on_device(ncol, x, am, pin, pm, pg, ls, fp, sp, ow, png, hw, bw):
    seqs, res, ch = x.shape
    cols, z = pin.shape[1:]
    cw = fp.shape[1]
    lanes = res * cw
    hid = hw.shape[1]
    jts = cols // res
    pairs = res * cols
    n = 2 * ncol
    outw = ow.shape[0]
    rows = outw // ncol
    srows = ch // 2 // n
    dma = pltpu.SemaphoreType.DMA
    vm = pltpu.VMEM
    scratch = [
        vm((2, seqs, lanes), BF16), vm((jts, 2, seqs, lanes), BF16), vm((8, lanes), F32),
        vm((2, 8, lanes), F32), vm((2, jts, 8, lanes), F32),
        vm((seqs, lanes), BF16), vm((seqs, lanes), BF16),
        vm((outw // lanes, pairs, lanes), F32), vm((lanes, lanes), BF16),
        vm((res * seqs, ch), F32), vm((res * seqs, ch), BF16),
        vm((2, jts, seqs, lanes), BF16), vm((ncol, seqs, lanes), BF16),
        vm((seqs, lanes), F32), vm((seqs, lanes), F32),
        vm((2, ncol, rows, z), BF16), vm((ncol, rows, z), BF16), vm((ncol, rows, z), BF16),
        vm((ncol, rows, z), BF16), vm((rows, z), BF16), vm((2, ncol, rows, z), BF16),
        vm((n, srows, 4 * cw), F32), vm((n, srows, 4 * cw), F32), vm((srows, 4 * cw), F32),
        vm((n, srows, 4 * cw), F32),
        dma, dma((jts, 2)), dma, dma((jts, 2)), dma((ncol,)), dma,
        dma, dma((ncol,)), dma((ncol,)), dma((ncol,)), dma((n,)), dma((n,)),
        dma, dma((ncol,)), dma, dma((ncol,)), dma((2, jts)), dma,
        dma, dma((ncol,)), dma((ncol,)), dma((ncol,)), dma((n,)), dma((n,)),
    ]
    spec = pl.BlockSpec(memory_space=pltpu.VMEM)
    feat, couple, wsum, small = pl.pallas_call(
        functools.partial(kernel, ncol, seqs, res, cols, cw),
        out_shape=(
            jax.ShapeDtypeStruct((res * seqs, ch), BF16),
            jax.ShapeDtypeStruct((pairs, z), BF16),
            jax.ShapeDtypeStruct((2 * outw, z), BF16),
            jax.ShapeDtypeStruct((ch // 2, 4 * cw), F32),
        ),
        in_specs=[spec] * 12,
        out_specs=(spec,) * 4,
        scratch_shapes=scratch,
        compiler_params=pltpu.CompilerParams(
            collective_id=0, has_side_effects=True, vmem_limit_bytes=60 << 20
        ),
    )(
        x.transpose(1, 0, 2).reshape(res * seqs, ch), am, pin.reshape(pairs, z), pm,
        pg.reshape(pairs, z), ls.reshape(1, ch), fp, sp, ow, png.reshape(1, z), hw, bw,
    )
    d1 = jnp.concatenate([small[:, :cw], small[:, 2 * cw : 3 * cw]], axis=0)
    d2 = jnp.concatenate([small[:, cw : 2 * cw], small[:, 3 * cw :]], axis=0)
    d_mid = wsum[outw : outw + hid].reshape(hid // z, z, z).transpose(1, 0, 2).reshape(z, hid)
    return (
        feat.reshape(res, seqs, ch).transpose(1, 0, 2),
        couple.reshape(res, cols, z),
        d1,
        d2,
        wsum[:outw].astype(F32),
        d_mid.astype(F32),
        wsum[outw + hid :].astype(F32),
    )


def solution(mesh):
    msa = P(("group", "depth"), "col")
    pair = P(("group", "col"), "depth")
    rep = P()
    part = P("group", None)
    return jax.shard_map(
        functools.partial(on_device, mesh.shape["col"]),
        mesh=mesh,
        in_specs=(msa, msa, pair, pair, pair) + (rep,) * 7,
        out_specs=(msa, pair, part, part, part, part, part),
        check_vma=False,
    )
```

time: 363 us -> 48.6 us (0.13)
  waiting for transfers between devices: 252 us -> 0 us
  blocking collectives: 57.5 us -> 0 us
  Pallas kernels: 0 us -> 36.9 us
  between operations: 14.8 us -> 0.67 us
  local copies, waits for them, and re-layouts: 20.5 us -> 7.69 us
  matrix products: 11.6 us -> 0 us
    psum x2 -> x0, waiting for transfers between devices: 186 us -> none  [on_device(): lax.psum((first_projector_derivative, second_projector_derivative, result...]
    unnamed x6 -> x0, waiting for transfers between devices: 66.5 us -> none
    all_gather x3 -> x0, blocking collectives: 55 us -> none  [the longest x1 32.6 us: on_device(): lax.all_gather(right_flat, 'col', axis=1, tiled=True)]
    pallas_call x0 -> x1, Pallas kernels: none -> 36.9 us  [on_device(): pl.pallas_call(functools.partial(kernel, ncol, seqs, res, cols, cw), out_...]
    dot_general x18 -> x0, matrix products: 11.6 us -> none  [the longest x1 1.8 us: partial_outer(): jnp.einsum('sic,sejd->iejcd', left_proj, right_piece, preferred_element_t...]
    unnamed x38 -> x12, local copies, waits for them, and re-layouts: 12.4 us -> 4.94 us
  transfers between devices with their start and end apart: 4 -> 0, of which waited for: 3 -> 0; matrix products, arithmetic and copies ran while one was open for 2% -> 0% of each run, Pallas kernels for 0% -> 0%
where the time goes in v1:
time: 48.6 us; the launch traced here: 48.2 us
  Pallas kernels  36.9 us (76%)
  local copies, waits for them, and re-layouts  7.69 us (16%)
  other arithmetic  2.94 us (6%)
  between operations  0.67 us (1%)
    pallas_call x1, Pallas kernels, on_device(): pl.pallas_call(functools.partial(kernel, ncol, seqs, res, cols, cw), out_...  36.9 us
    unnamed x12, local copies, waits for them, and re-layouts  4.94 us
    reshape x1, local copies, waits for them, and re-layouts, on_device(): feat.reshape(res, seqs, ch).transpose(1, 0, 2)  1.69 us

profile of v1, /device:TPU:0, one launch (start us, length us, event | category | flops | bytes accessed | tf_op | source)
XLA Modules:
  0.0 48.2 jit_solution(7511356373978814376)
XLA Ops:
  0.6 0.0 copy-start.2
  0.6 1.4 %copy.28.am_ref = s32[64,4]{1,0:T(8,128)} copy(s32[64,4]{0,1:T(4,128)} %param.13) | data formatting | bytes 2048 | tf_op args[1]
  2.1 1.4 %copy.29.fp_ref = bf16[256,32]{1,0:T(8,128)(2,1)} copy(bf16[256,32]{0,1:T(8,128)(2,1)} %param.18) | data formatting | bytes 32768 | tf_op args[6]
  3.5 1.4 %copy.30.sp_ref = bf16[256,32]{1,0:T(8,128)(2,1)} copy(bf16[256,32]{0,1:T(8,128)(2,1)} %param.19) | data formatting | bytes 32768 | tf_op args[7]
  5.0 0.0 copy-done.2
  5.0 0.7 %copy.27 = bf16[4,64,256]{2,1,0:T(8,128)(2,1)} copy(bf16[4,64,256]{2,0,1:T(4,128)(2,1)S(1)} %bitcast.21) | data formatting | bytes 262144 | tf_op jit(solution)/shard_map/transpose | solution.py:479
  5.6 36.9 %shard_map.171 = (bf16[256,256]{1,0:T(8,128)(2,1)}, bf16[64,128]{1,0:T(8,128)(2,1)}, bf16[2048,128]{1,0:T(8,128)(2,1)}, f32[128,128]{1,0:T(8,128)}) custom-call(bf16[256,256]{1,0:T(8,128)(2,1)} %bitcast.20, s32[64,4]{1,0:T(8,128)} %copy.28.am_ref, bf16[64,128]{1,0:T(8,128)(2,1)} %bitcast.24, s32[4,16]{1,0:T(4,128)} %pm_ref.1, bf16[64,128]{1,0:T(8,128)(2,1)} %bitcast.25, ...), custom_call_target="tpu_custom_call" | custom-call | tf_op jit(solution)/shard_map/pallas_call | solution.py:464
  42.5 0.0 copy-start
  42.6 1.7 %copy.40 = bf16[4,64,256]{2,0,1:T(4,128)(2,1)} copy(bf16[4,64,256]{2,1,0:T(8,128)(2,1)} %bitcast.23) | data formatting | bytes 262144 | tf_op jit(solution)/shard_map/reshape | solution.py:486
  44.2 0.0 copy-start.1
  44.2 0.0 copy-done
  44.3 0.1 fusion
  44.4 0.1 copy.34
  44.4 0.1 copy.35
  44.5 0.1 copy.33
  44.6 0.1 copy.32
  44.6 0.7 %pad_maximum_fusion = (f32[256,32]{0,1:T(8,128)}, f32[256,32]{0,1:T(8,128)}) fusion(f32[128,32]{0,1:T(8,128)S(1)} %copy.33, f32[128,32]{0,1:T(8,128)S(1)} %copy.32, f32[128,32]{0,1:T(8,128)S(1)} %copy.35, f32[128,32]{0,1:T(8,128)S(1)} %copy.34), kind=kLoop, calls=%fused_computation.5 | loop fusion | flops 16384 | bytes 131072 | tf_op jit(solution)/shard_map/concatenate | solution.py:482
  45.3 0.0 copy-done.1
  45.3 0.7 %slice_convert_fusion.1 = (f32[512,128]{1,0:T(8,128)}, bf16[512,128]{1,0:T(8,128)(2,1)S(1)}) fusion(bf16[2048,128]{1,0:T(8,128)(2,1)S(1)} %copy-done.1), kind=kLoop, calls=%fused_computation.4 | loop fusion | flops 65536 | bytes 655360 | tf_op jit(solution)/shard_map/convert_element_type | solution.py:492
  46.0 0.8 %slice_convert_fusion = f32[1024,128]{1,0:T(8,128)} fusion(bf16[2048,128]{1,0:T(8,128)(2,1)S(1)} %copy-done.1), kind=kLoop, calls=%fused_computation.2 | loop fusion | flops 131072 | bytes 786432 | tf_op jit(solution)/shard_map/convert_element_type | solution.py:490
  46.9 0.0 copy-start.3
  46.9 0.7 %copy_bitcast_fusion = f32[128,512]{1,0:T(8,128)} fusion(bf16[4,128,128]{2,1,0:T(8,128)(2,1)S(1)} %bitcast.19), kind=kLoop, calls=%fused_computation | loop fusion | flops 65536 | bytes 393216 | tf_op jit(solution)/shard_map/convert_element_type | solution.py:491
  47.6 0.0 copy-done.3
  47.6 0.6 %copy.42 = bf16[4,16,128]{2,1,0:T(8,128)(2,1)} copy(bf16[4,16,128]{2,1,0:T(8,128)(2,1)S(1)} %bitcast.26) | data formatting | bytes 32768
Async XLA Ops:
  0.6 4.3 %copy-start.2 = (bf16[64,4,256]{2,1,0:T(4,128)(2,1)S(1)}, bf16[64,4,256]{2,1,0:T(4,128)(2,1)}, u32[]{:S(2)}) copy-start(bf16[64,4,256]{2,1,0:T(4,128)(2,1)} %param.12) | copy-start | bytes 393220
  42.5 1.7 %copy-start = (f32[128,128]{1,0:T(8,128)S(1)}, f32[128,128]{1,0:T(8,128)}, u32[]{:S(2)}) copy-start(f32[128,128]{1,0:T(8,128)} %get-tuple-element.13) | copy-start | bytes 196612
  44.2 1.1 %copy-start.1 = (bf16[2048,128]{1,0:T(8,128)(2,1)S(1)}, bf16[2048,128]{1,0:T(8,128)(2,1)}, u32[]{:S(2)}) copy-start(bf16[2048,128]{1,0:T(8,128)(2,1)} %get-tuple-element.14) | copy-start | bytes 1572868
  46.9 0.7 %copy-start.3 = (bf16[64,128]{1,0:T(8,128)(2,1)S(1)}, bf16[64,128]{1,0:T(8,128)(2,1)}, u32[]{:S(2)}) copy-start(bf16[64,128]{1,0:T(8,128)(2,1)} %get-tuple-element.12) | copy-start | bytes 49156

commit v2 on v1

--- a/solution.py
+++ b/solution.py
@@ -72,7 +72,10 @@
             device_id=(g, d, c), device_id_type=MESH,
         )
 
-    scaled, inv = norm_pieces(x_ref[...].astype(F32))
+    rs_r = iota((res * seqs, res * seqs), 0)
+    rs_c = iota((res * seqs, res * seqs), 1)
+    by_res = (lax.rem(rs_r, seqs) * res + lax.div(rs_r, seqs) == rs_c).astype(F32).astype(BF16)
+    scaled, inv = norm_pieces(mm(by_res, x_ref[...].astype(F32).reshape(res * seqs, x_ref.shape[2]).astype(BF16)))
     normed = (scaled * ls_ref[...]).astype(BF16)
     scaled_sc[...] = scaled
     normed_sc[...] = normed
@@ -80,30 +83,31 @@
     el_l = iota((cw, lanes), 1)
     expand_l = (grp * lax.div(lax.rem(el_l, cw), res) + lax.div(el_l, cw) == el_c).astype(F32).astype(BF16)
     expand_r = (lax.rem(el_l, cw) == el_c).astype(F32).astype(BF16)
-    wl = mm(fp_ref[...], expand_l).astype(BF16)
-    wr = mm(sp_ref[...], expand_r).astype(BF16)
+    wl = mm(fp_ref[...], expand_l, 0, 0).astype(BF16)
+    wr = mm(sp_ref[...], expand_r, 0, 0).astype(BF16)
     pl_full = mm(normed, wl)
     pr_full = mm(normed, wr)
     ln = iota((seqs, lanes), 1)
     res_l = lax.rem(ln, res)
     res_r = lax.div(ln, cw)
-    mask = am_ref[...].astype(F32)
+    mask = am_ref[...].astype(F32).astype(BF16)
+    r_at = iota((res, lanes), 0)
+    l_at = iota((res, lanes), 1)
+    ml = mm(mask, (lax.rem(l_at, res) == r_at).astype(F32).astype(BF16), 0, 0)
+    mr = mm(mask, (lax.div(l_at, cw) == r_at).astype(F32).astype(BF16), 0, 0)
     zero = jnp.zeros((seqs, lanes), F32)
-    left, right, ml, mr, mpad = zero, zero, zero, zero, zero
+    left, right = zero, zero
     for r in range(res):
-        col = jnp.broadcast_to(mask[:, r : r + 1], (seqs, lanes))
         left = jnp.where(res_l == r, pl_full[r * seqs : (r + 1) * seqs], left)
         right = jnp.where(res_r == r, pr_full[r * seqs : (r + 1) * seqs], right)
-        ml = jnp.where(res_l == r, col, ml)
-        mr = jnp.where(res_r == r, col, mr)
-        mpad = jnp.where(ln == r, col, mpad)
     left = (left * ml).astype(BF16)
     right = (right * mr).astype(BF16)
     lsend[...] = left
     rsend[...] = right
     lbuf[e] = left
     eye = (iota((seqs, lanes), 0) == ln).astype(F32).astype(BF16)
-    mt = mm(mpad.astype(BF16), eye, 0, 0)[0:8]
+    grow = (iota((res, 8), 0) == iota((res, 8), 1)).astype(F32).astype(BF16)
+    mt = mm(grow, mm(mask, eye).astype(BF16), 0, 0)
     mloc[...] = mt
     mrow[e] = mt
     own_e = lax.div(k, jts)
@@ -213,6 +217,18 @@
     opm = (grad_mid / count).astype(BF16)
 
     rows = wb.shape[2]
+    d_out = mm(outer_b, opm, 0, 0).astype(BF16)
+    d_mid = mm(pnormed, grad_hidden, 0, 0).astype(BF16)
+    d_fin = mm(hidden, masked_grad, 0, 0).astype(BF16)
+    wb[0] = d_out.reshape(ncol, rows, z)
+    per = z // rows
+    for b in range(d_mid.shape[1] // z):
+        wb[1, b * per : (b + 1) * per] = d_mid[:, b * z : (b + 1) * z].reshape(per, rows, z)
+    half = (d_mid.shape[1] // z) * per
+    wb[1, half:] = d_fin.reshape(ncol - half, rows, z)
+    c_w1 = rcopy(wb.at[f], w1recv, snd_w1, sem_w1, f, k)
+    c_w1.start()
+
     g_out = mm(opm, ow_ref[...], 1, 1)
     tall = 2 * res
     perm_r = iota((cts * tall, cts * tall), 0)
@@ -276,17 +292,7 @@
     c_gl = rcopy(glsend, glrecv, snd_gl, sem_gl, f, k)
     c_gl.start()
 
-    d_out = mm(outer_b, opm, 0, 0).astype(BF16)
-    d_mid = mm(pnormed, grad_hidden, 0, 0).astype(BF16)
-    d_fin = mm(hidden, masked_grad, 0, 0).astype(BF16)
-    wb[0] = d_out.reshape(ncol, rows, z)
-    per = z // rows
-    for b in range(d_mid.shape[1] // z):
-        wb[1, b * per : (b + 1) * per] = d_mid[:, b * z : (b + 1) * z].reshape(per, rows, z)
-    half = (d_mid.shape[1] // z) * per
-    wb[1, half:] = d_fin.reshape(ncol - half, rows, z)
-    c_w1 = rcopy(wb.at[f], w1recv, snd_w1, sem_w1, f, k)
-    c_w1.start()
+
     c_w1.wait()
     w1s[...] = (wb[e].astype(F32) + w1recv[...].astype(F32)).astype(BF16)
 
@@ -308,23 +314,21 @@
         gr_sum = gr_sum + grrecv[kk].astype(F32)
     grad_r = (gr_sum * mr).astype(BF16).astype(F32)
     tw = 2 * cw
-    fold_l = iota((lanes, 2 * tw), 0)
-    fold_c = iota((lanes, 2 * tw), 1)
+    fold_l = iota((lanes, tw), 0)
+    fold_c = iota((lanes, tw), 1)
     c_of = grp * lax.div(lax.rem(fold_l, cw), res) + lax.div(fold_l, cw)
-    sel_l = (c_of == lax.rem(fold_c, tw)).astype(F32).astype(BF16)
-    sel_r = (lax.rem(fold_l, cw) + cw == lax.rem(fold_c, tw)).astype(F32).astype(BF16)
+    sel_l = (c_of == fold_c).astype(F32).astype(BF16)
+    sel_r = (lax.rem(fold_l, cw) + cw == fold_c).astype(F32).astype(BF16)
     gf = []
     for r in range(res):
         a = jnp.where(res_l == r, grad_l, 0.0).astype(BF16)
         b = jnp.where(res_r == r, grad_r, 0.0).astype(BF16)
         gf.append(mm(a, sel_l) + mm(b, sel_r))
-    gfold = jnp.concatenate(gf, axis=0)
-    low = iota(gfold.shape, 1) < tw
-    ga = jnp.where(low, gfold, 0.0).astype(BF16)
-    gb = jnp.where(low, 0.0, gfold).astype(BF16)
+    gfold = jnp.concatenate(gf, axis=0).astype(BF16)
     nrm = normed_sc[...]
+    d12 = mm(gfold, nrm, 0, 0)
     ch = nrm.shape[1] // 2
-    d12 = mm(nrm[:, :ch], ga, 0, 0) + mm(nrm[:, ch:], gb, 0, 0)
+    d12 = jnp.concatenate([d12[:, :ch], d12[:, ch:]], axis=0)
     sm[...] = d12.reshape(sm.shape)
 
     def s1_copy(t):
@@ -363,8 +367,12 @@
     w4_own = rcopy(w3, wout.at[e, k], snd_w4.at[k], sem_w4.at[k], f, k)
     w4_own.start()
 
-    nn = mm(ga[:, :cw], fp_ref[...], 1, 1) + mm(ga[:, cw:tw], sp_ref[...], 1, 1)
-    feat_ref[...] = standardize_adjoint(nn * ls_ref[...], scaled_sc[...], inv).astype(BF16)
+    nn = mm(gfold[:, :cw], fp_ref[...]) + mm(gfold[:, cw:], sp_ref[...])
+    feat = standardize_adjoint(nn * ls_ref[...], scaled_sc[...], inv).astype(BF16)
+    fr = iota((res * seqs, res * seqs), 0)
+    fc = iota((res * seqs, res * seqs), 1)
+    by_seq = (lax.rem(fr, res) * seqs + lax.div(fr, res) == fc).astype(F32).astype(BF16)
+    feat_ref[...] = mm(by_seq, feat).reshape(feat_ref.shape).astype(BF16)
 
     for p in range(n):
 
@@ -440,7 +448,7 @@
     n = 2 * ncol
     outw = ow.shape[0]
     rows = outw // ncol
-    srows = ch // 2 // n
+    srows = 4 * cw // n
     dma = pltpu.SemaphoreType.DMA
     vm = pltpu.VMEM
     scratch = [
@@ -453,8 +461,8 @@
         vm((seqs, lanes), F32), vm((seqs, lanes), F32),
         vm((2, ncol, rows, z), BF16), vm((ncol, rows, z), BF16), vm((ncol, rows, z), BF16),
         vm((ncol, rows, z), BF16), vm((rows, z), BF16), vm((2, ncol, rows, z), BF16),
-        vm((n, srows, 4 * cw), F32), vm((n, srows, 4 * cw), F32), vm((srows, 4 * cw), F32),
-        vm((n, srows, 4 * cw), F32),
+        vm((n, srows, ch // 2), F32), vm((n, srows, ch // 2), F32), vm((srows, ch // 2), F32),
+        vm((n, srows, ch // 2), F32),
         dma, dma((jts, 2)), dma, dma((jts, 2)), dma((ncol,)), dma,
         dma, dma((ncol,)), dma((ncol,)), dma((ncol,)), dma((n,)), dma((n,)),
         dma, dma((ncol,)), dma, dma((ncol,)), dma((2, jts)), dma,
@@ -464,10 +472,10 @@
     feat, couple, wsum, small = pl.pallas_call(
         functools.partial(kernel, ncol, seqs, res, cols, cw),
         out_shape=(
-            jax.ShapeDtypeStruct((res * seqs, ch), BF16),
+            jax.ShapeDtypeStruct((seqs, res, ch), BF16),
             jax.ShapeDtypeStruct((pairs, z), BF16),
             jax.ShapeDtypeStruct((2 * outw, z), BF16),
-            jax.ShapeDtypeStruct((ch // 2, 4 * cw), F32),
+            jax.ShapeDtypeStruct((4 * cw, ch // 2), F32),
         ),
         in_specs=[spec] * 12,
         out_specs=(spec,) * 4,
@@ -476,14 +484,14 @@
             collective_id=0, has_side_effects=True, vmem_limit_bytes=60 << 20
         ),
     )(
-        x.transpose(1, 0, 2).reshape(res * seqs, ch), am, pin.reshape(pairs, z), pm,
-        pg.reshape(pairs, z), ls.reshape(1, ch), fp, sp, ow, png.reshape(1, z), hw, bw,
+        x, am.T, pin.reshape(pairs, z), pm,
+        pg.reshape(pairs, z), ls.reshape(1, ch), fp.T, sp.T, ow, png.reshape(1, z), hw, bw,
     )
-    d1 = jnp.concatenate([small[:, :cw], small[:, 2 * cw : 3 * cw]], axis=0)
-    d2 = jnp.concatenate([small[:, cw : 2 * cw], small[:, 3 * cw :]], axis=0)
+    d1 = jnp.concatenate([small[:cw], small[2 * cw : 3 * cw]], axis=1).T
+    d2 = jnp.concatenate([small[cw : 2 * cw], small[3 * cw :]], axis=1).T
     d_mid = wsum[outw : outw + hid].reshape(hid // z, z, z).transpose(1, 0, 2).reshape(z, hid)
     return (
-        feat.reshape(res, seqs, ch).transpose(1, 0, 2),
+        feat,
         couple.reshape(res, cols, z),
         d1,
         d2,

time: 48.6 us -> 44.5 us (0.916)
  local copies, waits for them, and re-layouts: 7.69 us -> 2.38 us
  other arithmetic: 2.94 us -> 3.88 us
    unnamed x12 -> x8, local copies, waits for them, and re-layouts: 4.94 us -> 1.55 us
    reshape x1 -> x0, local copies, waits for them, and re-layouts: 1.69 us -> none  [on_device(): feat.reshape(res, seqs, ch).transpose(1, 0, 2)]
    convert_element_type x1, other arithmetic: 0.73 us -> 1.7 us  [on_device(): wsum[outw + hid:].astype(F32)]
    transpose x1 -> x0, local copies, waits for them, and re-layouts: 0.67 us -> none  [on_device(): x.transpose(1, 0, 2).reshape(res * seqs, ch)]
    concatenate x1 -> x0, other arithmetic: 0.66 us -> none  [on_device(): d1 = jnp.concatenate([small[:, :cw], small[:, 2 * cw:3 * cw]], axis=0)]
    transpose x0 -> x1, other arithmetic: none -> 0.63 us  [on_device(): d1 = jnp.concatenate([small[:cw], small[2 * cw:3 * cw]], axis=1).T]
where the time goes in v2:
time: 44.5 us; the launch traced here: 44.2 us
  Pallas kernels  37.2 us (84%)
  other arithmetic  3.88 us (9%)
  local copies, waits for them, and re-layouts  2.38 us (5%)
  between operations  0.66 us (1%)
    pallas_call x1, Pallas kernels, on_device(): pl.pallas_call(functools.partial(kernel, ncol, seqs, res, cols, cw), out_...  37.2 us
    convert_element_type x1, other arithmetic, on_device(): wsum[outw + hid:].astype(F32)  1.7 us
    unnamed x8, local copies, waits for them, and re-layouts  1.55 us

profile of v2, /device:TPU:0, one launch (start us, length us, event | category | flops | bytes accessed | tf_op | source)
XLA Modules:
  0.0 44.2 jit_solution(573650447133280142)
XLA Ops:
  0.6 37.2 %shard_map.171 = (bf16[64,4,256]{2,1,0:T(4,128)(2,1)}, bf16[64,128]{1,0:T(8,128)(2,1)}, bf16[2048,128]{1,0:T(8,128)(2,1)}, f32[128,128]{1,0:T(8,128)}) custom-call(bf16[64,4,256]{2,1,0:T(4,128)(2,1)} %x_ref.1, s32[4,64]{1,0:T(4,128)} %bitcast.26, bf16[64,128]{1,0:T(8,128)(2,1)} %bitcast.21, s32[4,16]{1,0:T(4,128)} %pm_ref.1, bf16[64,128]{1,0:T(8,128)(2,1)} %bitcast.22, ...), custom_call_target="tpu_custom_call" | custom-call | tf_op jit(solution)/shard_map/pallas_call | solution.py:472
  37.9 0.0 copy-start
  37.9 0.8 %fusion = (f32[32,128]{1,0:T(8,128)S(1)}, f32[32,128]{1,0:T(8,128)S(1)}, f32[32,128]{1,0:T(8,128)S(1)}, f32[32,128]{1,0:T(8,128)S(1)}) fusion(f32[128,128]{1,0:T(8,128)} %get-tuple-element.13), kind=kLoop, calls=%fused_computation.6 | loop fusion | bytes 131072 | tf_op jit(solution)/shard_map/slice | solution.py:491
  38.7 0.6 %maximum_bitcast_fusion = (f32[256,32]{0,1:T(8,128)}, f32[256,32]{0,1:T(8,128)}) fusion(f32[32,128]{1,0:T(8,128)S(1)} %get-tuple-element.19, f32[32,128]{1,0:T(8,128)S(1)} %get-tuple-element.20, f32[32,128]{1,0:T(8,128)S(1)} %get-tuple-element.18, f32[32,128]{1,0:T(8,128)S(1)} %get-tuple-element.17), kind=kLoop, calls=%fused_computation.4 | loop fusion | flops 16384 | bytes 131072 | tf_op jit(solution)/shard_map/transpose | solution.py:490
  39.4 1.7 %slice_convert_fusion.1 = (f32[512,128]{1,0:T(8,128)}, bf16[512,128]{1,0:T(8,128)(2,1)S(1)}) fusion(bf16[2048,128]{1,0:T(8,128)(2,1)} %get-tuple-element.14), kind=kLoop, calls=%fused_computation.3 | loop fusion | flops 65536 | bytes 655360 | tf_op jit(solution)/shard_map/convert_element_type | solution.py:500
  41.0 0.0 copy-done
  41.1 0.8 %slice_convert_fusion = f32[1024,128]{1,0:T(8,128)} fusion(bf16[2048,128]{1,0:T(8,128)(2,1)S(1)} %copy-done), kind=kLoop, calls=%fused_computation.2 | loop fusion | flops 131072 | bytes 786432 | tf_op jit(solution)/shard_map/convert_element_type | solution.py:498
  41.9 0.0 copy-start.1
  41.9 0.7 %copy_bitcast_fusion = f32[128,512]{1,0:T(8,128)} fusion(bf16[4,128,128]{2,1,0:T(8,128)(2,1)S(1)} %bitcast.20), kind=kLoop, calls=%fused_computation | loop fusion | flops 65536 | bytes 393216 | tf_op jit(solution)/shard_map/convert_element_type | solution.py:499
  42.6 0.2 copy-done.1
  42.8 0.0 copy-start.2
  42.8 0.7 %copy.24 = bf16[64,4,256]{2,1,0:T(4,128)(2,1)} copy(bf16[64,4,256]{2,1,0:T(4,128)(2,1)S(1)} %copy-done.1) | data formatting | bytes 262144
  43.5 0.1 copy-done.2
  43.6 0.6 %copy.25 = bf16[4,16,128]{2,1,0:T(8,128)(2,1)} copy(bf16[4,16,128]{2,1,0:T(8,128)(2,1)S(1)} %bitcast.25) | data formatting | bytes 32768
Async XLA Ops:
  37.9 3.2 %copy-start = (bf16[2048,128]{1,0:T(8,128)(2,1)S(1)}, bf16[2048,128]{1,0:T(8,128)(2,1)}, u32[]{:S(2)}) copy-start(bf16[2048,128]{1,0:T(8,128)(2,1)} %get-tuple-element.14) | copy-start | bytes 1572868
  41.9 1.0 %copy-start.1 = (bf16[64,4,256]{2,1,0:T(4,128)(2,1)S(1)}, bf16[64,4,256]{2,1,0:T(4,128)(2,1)}, u32[]{:S(2)}) copy-start(bf16[64,4,256]{2,1,0:T(4,128)(2,1)} %get-tuple-element.30) | copy-start | bytes 393220
  42.8 0.7 %copy-start.2 = (bf16[64,128]{1,0:T(8,128)(2,1)S(1)}, bf16[64,128]{1,0:T(8,128)(2,1)}, u32[]{:S(2)}) copy-start(bf16[64,128]{1,0:T(8,128)(2,1)} %get-tuple-element.12) | copy-start | bytes 49156
